TPU v7x, 32 devices: a whole 2x2x4 slice. The times are simulated.
32 devices in a mesh: rep: 8 (over y, x, core), shard: 4 (over z).
Axes of the slice: x: 2, y: 2, z: 4, core: 2. Of those that a mesh axis runs over, the one named last changes fastest.
Arguments:
- inputs: bfloat16 [8, 4, 1104, 1024], P('rep', 'shard'), may hold values from -6 to 6
- counts: int32 [8], P('rep'), may hold values from 1 to 4, as said below
- ln1_gain: bfloat16 [1024], P('shard'), may hold values from 0.5 to 1.5
- ln1_shift: bfloat16 [1024], P('shard'), may hold values from -4 to 4
- w_qkv: bfloat16 [1024, 3072], P('shard'), may hold values from -0.1875 to 0.1875
- qv_bias: bfloat16 [2048], P('shard'), may hold values from -4 to 4
- w_out: bfloat16 [1024, 1024], P('shard'), may hold values from -0.75 to 0.75
- out_bias: bfloat16 [1024], P('shard'), may hold values from -4 to 4
- ln2_gain: bfloat16 [1024], P('shard'), may hold values from 0.5 to 1.5
- ln2_shift: bfloat16 [1024], P('shard'), may hold values from -4 to 4
- w_up: bfloat16 [1024, 4096], P('shard'), may hold values from -0.1875 to 0.1875
- up_bias: bfloat16 [4096], P('shard'), may hold values from -4 to 4
- w_down: bfloat16 [4096, 1024], P('shard'), may hold values from -0.09375 to 0.09375
- down_bias: bfloat16 [1024], P('shard'), may hold values from -4 to 4
- cotangent: bfloat16 [8, 4, 1104, 1024], P('rep', 'shard'), may hold values from -6 to 6
Outputs:
- output: bfloat16 [8, 4, 1104, 1024], P('rep', 'shard')
- input_grad: float32 [8, 4, 1104, 1024], P('rep', 'shard')
- grad_ln1_gain: float32 [1024], P('shard')
- grad_ln1_shift: float32 [1024], P('shard')
- grad_w_qkv: float32 [1024, 3072], P('shard')
- grad_qv_bias: float32 [2048], P('shard')
- grad_w_out: float32 [1024, 1024], P('shard')
- grad_out_bias: float32 [1024], P('shard')
- grad_ln2_gain: float32 [1024], P('shard')
- grad_ln2_shift: float32 [1024], P('shard')
- grad_w_up: float32 [1024, 4096], P('shard')
- grad_up_bias: float32 [4096], P('shard')
- grad_w_down: float32 [4096, 1024], P('shard')
- grad_down_bias: float32 [1024], P('shard')
Inputs may be any that keep to these rules, and one draw needn't show every extreme that they name: A group's live sequences occupy its slots 0 to counts - 1; some group has exactly 4 and some exactly 1.
All inputs are finite; a program needn't handle non-finite values.
Results may differ from a plain program's by a relative error of at most 0.018.
Values may be sent and summed in bfloat16 or wider, within the bound.
No kernel may reach another device: no remote copies, remote signals or barrier semaphores. Data moves between devices by JAX's collectives and lax.ppermute only.
A program may use at most 256 MiB of HBM per device.

v0:
```python
import jax
import jax.numpy as jnp
from jax import lax
from jax.sharding import PartitionSpec as P

HEADS = 16
HDIM = 64
eps = 1e-06
head_block = 4


def layer_norm(values, gain, shift):
    centre = values - jnp.mean(values, -1, keepdims=True)
    spread = jnp.mean(centre * centre, -1, keepdims=True)
    return centre * lax.rsqrt(spread + eps) * gain + shift


def gelu_exact(values):
    return jax.nn.gelu(values, approximate=False)


def matmul(left, right):
    return jnp.dot(left, right, preferred_element_type=jnp.float32)


def left_trans(left, right):
    return lax.dot_general(
        left, right, (((0,), (0,)), ((), ())), preferred_element_type=jnp.float32
    )


def right_trans(left, right):
    return lax.dot_general(
        left, right, (((1,), (1,)), ((), ())), preferred_element_type=jnp.float32
    )


def body(
    inputs,
    counts,
    ln1_gain,
    ln1_shift,
    w_qkv,
    qv_bias,
    w_out,
    out_bias,
    ln2_gain,
    ln2_shift,
    w_up,
    up_bias,
    w_down,
    down_bias,
    cotangent,
):
    gathered = (
        lax.all_gather(ln1_gain, "shard", axis=0, tiled=True),
        lax.all_gather(ln1_shift, "shard", axis=0, tiled=True),
        lax.all_gather(w_qkv, "shard", axis=0, tiled=True),
        lax.all_gather(qv_bias, "shard", axis=0, tiled=True),
        lax.all_gather(w_out, "shard", axis=0, tiled=True),
        lax.all_gather(out_bias, "shard", axis=0, tiled=True),
        lax.all_gather(ln2_gain, "shard", axis=0, tiled=True),
        lax.all_gather(ln2_shift, "shard", axis=0, tiled=True),
        lax.all_gather(w_up, "shard", axis=0, tiled=True),
        lax.all_gather(up_bias, "shard", axis=0, tiled=True),
        lax.all_gather(w_down, "shard", axis=0, tiled=True),
        lax.all_gather(down_bias, "shard", axis=0, tiled=True),
    )
    (
        full_g1,
        full_s1,
        full_qkv,
        full_qvb,
        full_wout,
        full_bout,
        full_g2,
        full_s2,
        full_wup,
        full_bup,
        full_wdown,
        full_bdown,
    ) = gathered
    slots = inputs.shape[1]
    seq_len = inputs.shape[2]
    width = inputs.shape[3]
    n_rows = slots * seq_len
    groups = HEADS // head_block
    scale = HDIM ** (-0.5)
    first_slot = lax.axis_index("shard") * slots
    alive = (jnp.arange(slots, dtype=jnp.int32) + first_slot < counts[0]).astype(jnp.float32)
    alive_rows = jnp.broadcast_to(alive[:, None], (slots, seq_len)).reshape(n_rows, 1)
    tokens = inputs.reshape(n_rows, width).astype(jnp.float32)
    hidden_one, norm_one_back = jax.vjp(
        layer_norm, tokens, full_g1.astype(jnp.float32), full_s1.astype(jnp.float32)
    )
    hidden_one_b = hidden_one.astype(jnp.bfloat16)
    projected = matmul(hidden_one_b, full_qkv)
    bias_f = full_qvb.astype(jnp.float32)
    queries_b = (projected[:, :width] + bias_f[:width]).astype(jnp.bfloat16)
    keys_b = projected[:, width : 2 * width].astype(jnp.bfloat16)
    values_b = (projected[:, 2 * width :] + bias_f[width:]).astype(jnp.bfloat16)

    def arrange(values):
        return values.reshape(slots, seq_len, groups, head_block, HDIM).transpose(2, 0, 1, 3, 4)

    def restore(values):
        return values.transpose(1, 2, 0, 3, 4).reshape(n_rows, width)

    query_groups = arrange(queries_b)
    key_groups = arrange(keys_b)
    value_groups = arrange(values_b)

    def forward_group(operands):
        query_part, key_part, value_part = operands
        scores = (
            jnp.einsum("cqhd,ckhd->chqk", query_part, key_part, preferred_element_type=jnp.float32)
            * scale
        )
        largest = jnp.max(scores, -1, keepdims=True)
        exponent = jnp.exp(scores - largest)
        denominator = jnp.sum(exponent, -1, keepdims=True)
        probs_b = (exponent / denominator).astype(jnp.bfloat16)
        mixed = jnp.einsum(
            "chqk,ckhd->cqhd", probs_b, value_part, preferred_element_type=jnp.float32
        )
        return (mixed, (largest + jnp.log(denominator))[..., 0])

    mixed_groups, log_totals = lax.map(forward_group, (query_groups, key_groups, value_groups))
    attended_b = restore(mixed_groups).astype(jnp.bfloat16)
    middle = tokens + matmul(attended_b, full_wout) + full_bout.astype(jnp.float32)
    hidden_two, norm_two_back = jax.vjp(
        layer_norm, middle, full_g2.astype(jnp.float32), full_s2.astype(jnp.float32)
    )
    hidden_two_b = hidden_two.astype(jnp.bfloat16)
    pre_act = matmul(hidden_two_b, full_wup) + full_bup.astype(jnp.float32)
    activated, gelu_back = jax.vjp(gelu_exact, pre_act)
    activated_b = activated.astype(jnp.bfloat16)
    result = middle + matmul(activated_b, full_wdown) + full_bdown.astype(jnp.float32)
    output = (alive_rows * result).astype(jnp.bfloat16).reshape(inputs.shape)
    again = (
        lax.all_gather(ln1_gain, "shard", axis=0, tiled=True),
        lax.all_gather(ln1_shift, "shard", axis=0, tiled=True),
        lax.all_gather(w_qkv, "shard", axis=0, tiled=True),
        lax.all_gather(qv_bias, "shard", axis=0, tiled=True),
        lax.all_gather(w_out, "shard", axis=0, tiled=True),
        lax.all_gather(out_bias, "shard", axis=0, tiled=True),
        lax.all_gather(ln2_gain, "shard", axis=0, tiled=True),
        lax.all_gather(ln2_shift, "shard", axis=0, tiled=True),
        lax.all_gather(w_up, "shard", axis=0, tiled=True),
        lax.all_gather(up_bias, "shard", axis=0, tiled=True),
        lax.all_gather(w_down, "shard", axis=0, tiled=True),
        lax.all_gather(down_bias, "shard", axis=0, tiled=True),
    )
    back_qkv = again[2]
    back_wout = again[4]
    back_wup = again[8]
    back_wdown = again[10]
    d_out = alive_rows * cotangent.reshape(n_rows, width).astype(jnp.float32)
    d_out_b = d_out.astype(jnp.bfloat16)
    grad_wdown = left_trans(activated_b, d_out_b)
    grad_bdown = jnp.sum(d_out, 0)
    d_act = right_trans(d_out_b, back_wdown)
    d_pre_b = gelu_back(d_act)[0].astype(jnp.bfloat16)
    grad_wup = left_trans(hidden_two_b, d_pre_b)
    grad_bup = jnp.sum(d_pre_b.astype(jnp.float32), 0)
    d_hidden_two = right_trans(d_pre_b, back_wup)
    d_mid_norm, grad_g2, grad_s2 = norm_two_back(d_hidden_two)
    d_mid = d_out + d_mid_norm
    d_proj_b = d_mid.astype(jnp.bfloat16)
    grad_wout = left_trans(attended_b, d_proj_b)
    grad_bout = jnp.sum(d_proj_b.astype(jnp.float32), 0)
    d_att_b = right_trans(d_proj_b, back_wout).astype(jnp.bfloat16)
    d_att_groups = arrange(d_att_b)

    def backward_group(operands):
        query_part, key_part, value_part, log_total, grad_part = operands
        scores = (
            jnp.einsum("cqhd,ckhd->chqk", query_part, key_part, preferred_element_type=jnp.float32)
            * scale
        )
        attn_probs = jnp.exp(scores - log_total[..., None])
        probs_b = attn_probs.astype(jnp.bfloat16)
        d_probs = jnp.einsum(
            "cqhd,ckhd->chqk", grad_part, value_part, preferred_element_type=jnp.float32
        )
        row_inner = jnp.sum(d_probs * attn_probs, -1, keepdims=True)
        d_scores_b = (attn_probs * (d_probs - row_inner)).astype(jnp.bfloat16)
        d_query = (
            jnp.einsum("chqk,ckhd->cqhd", d_scores_b, key_part, preferred_element_type=jnp.float32)
            * scale
        )
        d_key = (
            jnp.einsum(
                "chqk,cqhd->ckhd", d_scores_b, query_part, preferred_element_type=jnp.float32
            )
            * scale
        )
        d_value = jnp.einsum(
            "chqk,cqhd->ckhd", probs_b, grad_part, preferred_element_type=jnp.float32
        )
        return (d_query, d_key, d_value)

    d_query_groups, d_key_groups, d_value_groups = lax.map(
        backward_group, (query_groups, key_groups, value_groups, log_totals, d_att_groups)
    )
    d_qkv_b = jnp.concatenate(
        [restore(d_query_groups), restore(d_key_groups), restore(d_value_groups)], 1
    ).astype(jnp.bfloat16)
    grad_qkv = left_trans(hidden_one_b, d_qkv_b)
    column_sums = jnp.sum(d_qkv_b.astype(jnp.float32), 0)
    grad_qvb = jnp.concatenate([column_sums[:width], column_sums[2 * width :]])
    d_hidden_one = right_trans(d_qkv_b, back_qkv)
    d_in_norm, grad_g1, grad_s1 = norm_one_back(d_hidden_one)
    input_grad = (d_mid + d_in_norm).reshape(inputs.shape)
    owned = (
        lax.psum_scatter(
            grad_g1.astype(jnp.bfloat16), "shard", scatter_dimension=0, tiled=True
        ).astype(jnp.float32),
        lax.psum_scatter(
            grad_s1.astype(jnp.bfloat16), "shard", scatter_dimension=0, tiled=True
        ).astype(jnp.float32),
        lax.psum_scatter(
            grad_qkv.astype(jnp.bfloat16), "shard", scatter_dimension=0, tiled=True
        ).astype(jnp.float32),
        lax.psum_scatter(
            grad_qvb.astype(jnp.bfloat16), "shard", scatter_dimension=0, tiled=True
        ).astype(jnp.float32),
        lax.psum_scatter(
            grad_wout.astype(jnp.bfloat16), "shard", scatter_dimension=0, tiled=True
        ).astype(jnp.float32),
        lax.psum_scatter(
            grad_bout.astype(jnp.bfloat16), "shard", scatter_dimension=0, tiled=True
        ).astype(jnp.float32),
        lax.psum_scatter(
            grad_g2.astype(jnp.bfloat16), "shard", scatter_dimension=0, tiled=True
        ).astype(jnp.float32),
        lax.psum_scatter(
            grad_s2.astype(jnp.bfloat16), "shard", scatter_dimension=0, tiled=True
        ).astype(jnp.float32),
        lax.psum_scatter(
            grad_wup.astype(jnp.bfloat16), "shard", scatter_dimension=0, tiled=True
        ).astype(jnp.float32),
        lax.psum_scatter(
            grad_bup.astype(jnp.bfloat16), "shard", scatter_dimension=0, tiled=True
        ).astype(jnp.float32),
        lax.psum_scatter(
            grad_wdown.astype(jnp.bfloat16), "shard", scatter_dimension=0, tiled=True
        ).astype(jnp.float32),
        lax.psum_scatter(
            grad_bdown.astype(jnp.bfloat16), "shard", scatter_dimension=0, tiled=True
        ).astype(jnp.float32),
    )
    o_g1, o_s1, o_qkv, o_qvb, o_wout, o_bout, o_g2, o_s2, o_wup, o_bup, o_wdown, o_bdown = owned
    summed = (
        lax.psum(o_g1.astype(jnp.bfloat16), "rep").astype(jnp.float32),
        lax.psum(o_s1.astype(jnp.bfloat16), "rep").astype(jnp.float32),
        lax.psum(o_qkv.astype(jnp.bfloat16), "rep").astype(jnp.float32),
        lax.psum(o_qvb.astype(jnp.bfloat16), "rep").astype(jnp.float32),
        lax.psum(o_wout.astype(jnp.bfloat16), "rep").astype(jnp.float32),
        lax.psum(o_bout.astype(jnp.bfloat16), "rep").astype(jnp.float32),
        lax.psum(o_g2.astype(jnp.bfloat16), "rep").astype(jnp.float32),
        lax.psum(o_s2.astype(jnp.bfloat16), "rep").astype(jnp.float32),
        lax.psum(o_wup.astype(jnp.bfloat16), "rep").astype(jnp.float32),
        lax.psum(o_bup.astype(jnp.bfloat16), "rep").astype(jnp.float32),
        lax.psum(o_wdown.astype(jnp.bfloat16), "rep").astype(jnp.float32),
        lax.psum(o_bdown.astype(jnp.bfloat16), "rep").astype(jnp.float32),
    )
    return (
        output,
        input_grad,
        summed[0],
        summed[1],
        summed[2],
        summed[3],
        summed[4],
        summed[5],
        summed[6],
        summed[7],
        summed[8],
        summed[9],
        summed[10],
        summed[11],
    )


def solution(mesh):
    placed = (
        P("rep", "shard", None, None),
        P("rep"),
        P("shard"),
        P("shard"),
        P("shard", None),
        P("shard"),
        P("shard", None),
        P("shard"),
        P("shard"),
        P("shard"),
        P("shard", None),
        P("shard"),
        P("shard", None),
        P("shard"),
        P("rep", "shard", None, None),
    )
    return jax.shard_map(
        body,
        mesh=mesh,
        in_specs=placed,
        out_specs=(
            P("rep", "shard", None, None),
            P("rep", "shard", None, None),
            P("shard"),
            P("shard"),
            P("shard", None),
            P("shard"),
            P("shard", None),
            P("shard"),
            P("shard"),
            P("shard"),
            P("shard", None),
            P("shard"),
            P("shard", None),
            P("shard"),
        ),
        check_vma=False,
    )
```

profile of v0, /device:TPU:0, one launch (start us, length us, event | category | flops | bytes accessed | tf_op | source)
XLA Modules:
  0.0 1330.5 jit_solution(4466956774392505986)
XLA Ops:
  53.3 14.0 %all-gather = bf16[4,1,256]{2,1,0:T(2,128)(2,1)S(1)} all-gather(bf16[1,1,256]{2,1,0:T(2,128)(2,1)S(1)} %reshape.260), channel_id=1, replica_groups=mesh['rep'=8,'shard'=4] {'shard'}, dimensions={0}, use_global_device_ids=true | all-gather | bytes 2560 | tf_op jit(solution)/shard_map/all_gather | solution.py:56
  79.4 16.0 %all_gather.49 = bf16[4096]{0:T(1024)(128)(2,1)S(1)} all-gather(bf16[1024]{0:T(1024)(128)(2,1)S(1)} %copy-done.47), channel_id=1, replica_groups=mesh['rep'=8,'shard'=4] {'shard'}, dimensions={0}, use_global_device_ids=true | all-gather | bytes 10240 | tf_op jit(solution)/shard_map/all_gather | solution.py:65
  97.8 30.4 %all-gather.12.cloned.1.call-done = bf16[1024,3072]{1,0:T(8,128)(2,1)} async-done(((bf16[256,3072]{1,0:T(8,128)(2,1)}), bf16[1024,3072]{1,0:T(8,128)(2,1)}) %all-gather.12.cloned.1.call-update) | async-done | bytes 6291472 | tf_op jit(solution)/shard_map/all_gather | solution.py:58
  156.2 131.5 %while.26 = (s32[]{:T(128)}, bf16[4,1,1104,4,64]{2,4,3,1,0:T(8,128)(2,1)}, f32[4,1,4,1104]{3,2,1,0:T(4,128)}, bf16[4,1,1104,4,64]{2,4,3,1,0:T(8,128)(2,1)}, bf16...) while((s32[]{:T(128)}, bf16[4,1,1104,4,64]{2,4,3,1,0:T(8,128)(2,1)}, ...), condition=%wide.region_5.6_spmd, body=%wide.region_2.5_spmd.sunk | while | flops 1282190080 | bytes 62444376 | solution.py:128
  297.9 26.0 %all-gather.16.cloned.1.call-done = bf16[1024,4096]{1,0:T(8,128)(2,1)} async-done(((bf16[256,4096]{1,0:T(8,128)(2,1)}), bf16[1024,4096]{1,0:T(8,128)(2,1)}) %all-gather.16.cloned.1.call-update) | async-done | bytes 8388624 | tf_op jit(solution)/shard_map/all_gather | solution.py:64
  323.9 54.4 %multiply_convert_fusion.1 = (bf16[1104,4096]{1,0:T(8,128)(2,1)}, f32[1104,4096]{1,0:T(8,128)}, f32[1104,4096]{1,0:T(8,128)}) fusion(f32[4096]{0:T(1024)S(1)} %copy-done.39, bf16[1024,4096]{1,0:T(8,128)(2,1)} %all-gather.16.cloned.1.call-done, f32[1104,1024]{1,0:T(8,128)} %copy-done.8, f32[1024]{0:T(1024)S(1)} %bitcast.254, f32[1024]{0:T(1024)S(1)} %bitcast.248, ...), kind=kOutput, calls=%fused_computation.56 | convolution fusion | flops 9565126656 | bytes 58163840 | tf_op jit(solution)/shard_map/dot_general | solution.py:23
  378.3 94.9 %all-gather.18.cloned.1.call-done = bf16[4096,1024]{1,0:T(8,128)(2,1)} async-done(((bf16[1024,1024]{1,0:T(8,128)(2,1)}), bf16[4096,1024]{1,0:T(8,128)(2,1)}) %all-gather.18.cloned.1.call-update) | async-done | bytes 8388624 | tf_op jit(solution)/shard_map/all_gather | solution.py:66
  473.2 25.4 %fusion.92 = (bf16[4096]{0:T(1024)(128)(2,1)}, bf16[1104,4096]{1,0:T(8,128)(2,1)}) fusion(f32[1104,4096]{1,0:T(8,128)} %get-tuple-element.193, f32[1104,4096]{1,0:T(8,128)} %get-tuple-element.206, bf16[4096,1024]{1,0:T(8,128)(2,1)} %all-gather.18.cloned.1.call-done, bf16[1,1,1104,1024]{3,2,1,0:T(8,128)(2,1)S(1)} %copy-done.6, f32[]{:T(128)} %bitcast.22), kind=kOutput, calls=%fused_computation.137 | convolution fusion | flops 9332240384 | bytes 55877636 | tf_op jit(solution)/shard_map/dot_general | solution.py:33
  498.6 18.1 %multiply_reduce_fusion.1 = (bf16[1024]{0:T(1024)(128)(2,1)}, f32[1104]{0:T(1024)S(1)}, bf16[1024]{0:T(1024)(128)(2,1)}, f32[1104,1024]{1,0:T(8,128)S(1)}) fusion(f32[1104,1024]{1,0:T(8,128)} %copy-done.8, f32[1104]{0:T(1024)S(1)} %fusion.76, f32[1104]{0:T(1024)S(1)} %broadcast_multiply_fusion, f32[1024]{0:T(1024)S(1)} %bitcast.249, ...), kind=kOutput, calls=%fused_computation.102 | convolution fusion | flops 9270064128 | bytes 26497984 | tf_op jit(solution)/shard_map/dot_general | solution.py:33
  538.8 243.8 %while.27 = (s32[]{:T(128)}, bf16[4,1,1104,4,64]{2,4,3,1,0:T(8,128)(2,1)}, bf16[4,1,1104,4,64]{2,4,3,1,0:T(8,128)(2,1)}, bf16[4,1,1104,4,64]{2,4,3,1,0:T(8,128)(...) while((s32[]{:T(128)}, ...), condition=%wide.region_12.13_spmd, body=%wide.region_10.12_spmd.sunk | while | flops 3159731968 | bytes 219023680 | solution.py:203
  560.7 17.6 %multiply_reduce_fusion.5 = (f32[4,1104]{1,0:T(4,128)S(1)}, f32[4,1104,1104]{1,2,0:T(8,128)}) fusion(f32[4,1104,1104]{1,2,0:T(8,128)} %fusion.140, bf16[4,1,1104,4,64]{2,4,3,1,0:T(8,128)(2,1)} %get-tuple-element.360, s32[]{:T(128)S(6)} %copy.89, bf16[4,1,1104,4,64]{2,4,3,1,0:T(8,128)(2,1)S(1)} %copy-done.5), kind=kOutput, calls=%fused_computation.20.clone.1 | convolution fusion | flops 633779904 | bytes 41048320 | tf_op jit(solution)/shard_map/while/body/eval_jaxpr/cqhd,ckhd->chqk/dot_general | solution.py:183
  578.4 13.5 %multiply_convert_fusion.3 = bf16[4,1104,1104]{1,2,0:T(8,128)(2,1)S(1)} fusion(f32[4,1104,1104]{1,2,0:T(8,128)} %fusion.140, f32[4,1104,1104]{1,2,0:T(8,128)} %get-tuple-element.309, f32[4,1104]{1,0:T(4,128)S(1)} %get-tuple-element.310), kind=kLoop, calls=%fused_computation.19.clone.1 | loop fusion | flops 14625792 | bytes 48770304 | tf_op jit(solution)/shard_map/while/body/eval_jaxpr/convert_element_type | solution.py:187
  621.6 17.5 %multiply_reduce_fusion.5 = (f32[4,1104]{1,0:T(4,128)S(1)}, f32[4,1104,1104]{1,2,0:T(8,128)}) fusion(f32[4,1104,1104]{1,2,0:T(8,128)} %fusion.140, bf16[4,1,1104,4,64]{2,4,3,1,0:T(8,128)(2,1)} %get-tuple-element.360, s32[]{:T(128)S(6)} %copy.89, bf16[4,1,1104,4,64]{2,4,3,1,0:T(8,128)(2,1)S(1)} %copy-done.5), kind=kOutput, calls=%fused_computation.20.clone.1 | convolution fusion | flops 633779904 | bytes 41048320 | tf_op jit(solution)/shard_map/while/body/eval_jaxpr/cqhd,ckhd->chqk/dot_general | solution.py:183
  639.2 13.5 %multiply_convert_fusion.3 = bf16[4,1104,1104]{1,2,0:T(8,128)(2,1)S(1)} fusion(f32[4,1104,1104]{1,2,0:T(8,128)} %fusion.140, f32[4,1104,1104]{1,2,0:T(8,128)} %get-tuple-element.309, f32[4,1104]{1,0:T(4,128)S(1)} %get-tuple-element.310), kind=kLoop, calls=%fused_computation.19.clone.1 | loop fusion | flops 14625792 | bytes 48770304 | tf_op jit(solution)/shard_map/while/body/eval_jaxpr/convert_element_type | solution.py:187
  682.5 17.5 %multiply_reduce_fusion.5 = (f32[4,1104]{1,0:T(4,128)S(1)}, f32[4,1104,1104]{1,2,0:T(8,128)}) fusion(f32[4,1104,1104]{1,2,0:T(8,128)} %fusion.140, bf16[4,1,1104,4,64]{2,4,3,1,0:T(8,128)(2,1)} %get-tuple-element.360, s32[]{:T(128)S(6)} %copy.89, bf16[4,1,1104,4,64]{2,4,3,1,0:T(8,128)(2,1)S(1)} %copy-done.5), kind=kOutput, calls=%fused_computation.20.clone.1 | convolution fusion | flops 633779904 | bytes 41048320 | tf_op jit(solution)/shard_map/while/body/eval_jaxpr/cqhd,ckhd->chqk/dot_general | solution.py:183
  743.3 17.5 %multiply_reduce_fusion.5 = (f32[4,1104]{1,0:T(4,128)S(1)}, f32[4,1104,1104]{1,2,0:T(8,128)}) fusion(f32[4,1104,1104]{1,2,0:T(8,128)} %fusion.140, bf16[4,1,1104,4,64]{2,4,3,1,0:T(8,128)(2,1)} %get-tuple-element.360, s32[]{:T(128)S(6)} %copy.89, bf16[4,1,1104,4,64]{2,4,3,1,0:T(8,128)(2,1)S(1)} %copy-done.5), kind=kOutput, calls=%fused_computation.20.clone.1 | convolution fusion | flops 633779904 | bytes 41048320 | tf_op jit(solution)/shard_map/while/body/eval_jaxpr/cqhd,ckhd->chqk/dot_general | solution.py:183
  782.6 15.3 %convolution_convert_fusion.2 = bf16[1024,3072]{1,0:T(8,128)(2,1)} fusion(bf16[1,1,1104,1024]{3,2,1,0:T(8,128)(2,1)} %param.19, f32[1024]{0:T(1024)S(1)} %bitcast.257, f32[1024]{0:T(1024)S(1)} %bitcast.244, f32[1104]{0:T(1024)S(1)} %copy-done.24, f32[1104]{0:T(1024)S(1)} %copy-done.22, bf16[1104,1024]{0,1:T(8,128)(2,1)} %bitcast.232, ...), kind=kOutput, calls=%fused_computation.75 | convolution fusion | flops 6976045056 | bytes 15352448 | tf_op jit(solution)/shard_map/dot_general | solution.py:27
  798.6 18.7 %convolution_convert_fusion.1 = bf16[1024,4096]{1,0:T(8,128)(2,1)} fusion(bf16[1104,4096]{1,0:T(8,128)(2,1)} %get-tuple-element.210, f32[1104,1024]{1,0:T(8,128)} %copy-done.8, f32[1024]{0:T(1024)S(1)} %bitcast.255, f32[1024]{0:T(1024)S(1)} %bitcast.251, f32[1104]{0:T(1024)S(1)} %copy-done.36, f32[1104]{0:T(1024)S(1)} %copy-done.26), kind=kOutput, calls=%fused_computation.71 | convolution fusion | flops 9270870016 | bytes 21971584 | tf_op jit(solution)/shard_map/dot_general | solution.py:27
  818.9 17.4 %convolution_convert_fusion = bf16[4096,1024]{1,0:T(8,128)(2,1)} fusion(bf16[1104,4096]{1,0:T(8,128)(2,1)} %get-tuple-element.192, bf16[1,1,1104,1024]{3,2,1,0:T(8,128)(2,1)S(1)} %copy-done.7, f32[]{:T(128)} %bitcast.22), kind=kOutput, calls=%fused_computation.70 | convolution fusion | flops 9268609024 | bytes 19693572 | tf_op jit(solution)/shard_map/dot_general | solution.py:27
  872.0 22.2 %all-reduce.10 = (bf16[1024]{0:T(1024)(128)(2,1)S(1)}, bf16[1024]{0:T(1024)(128)(2,1)S(1)}, bf16[2048]{0:T(1024)(128)(2,1)S(1)}, bf16[1024]{0:T(1024)(128)(2,1)S...) all-reduce(bf16[1024]{0:T(1024)(128)(2,1)S(1)} %get-tuple-element.1, ...), channel_id=2, replica_groups=mesh['rep'=8,'shard'=4] {'shard'}, use_global_device_ids=true, to_apply=%region_16.17.clone | all-reduce | flops 12288 | bytes 49152
  911.8 143.8 %reduce-scatter.9.cloned.1.call-done = bf16[256,4096]{1,0:T(8,128)(2,1)} async-done(((bf16[1024,4096]{1,0:T(8,128)(2,1)}), bf16[256,4096]{1,0:T(8,128)(2,1)}) %reduce-scatter.9.cloned.1.call-update) | async-done | bytes 2097168 | tf_op jit(solution)/shard_map/reduce_scatter | solution.py:240
  1055.6 147.7 %reduce-scatter.11.cloned.1.call-done = bf16[1024,1024]{1,0:T(8,128)(2,1)} async-done(((bf16[4096,1024]{1,0:T(8,128)(2,1)}), bf16[1024,1024]{1,0:T(8,128)(2,1)}) %reduce-scatter.11.cloned.1.call-update) | async-done | bytes 2097168 | tf_op jit(solution)/shard_map/reduce_scatter | solution.py:246
  1210.1 17.3 %fusion.72 = bf16[1,1,1104,1024]{3,2,1,0:T(8,128)(2,1)} fusion(f32[1104,1024]{1,0:T(8,128)} %copy-done.8, bf16[1104,4096]{1,0:T(8,128)(2,1)} %get-tuple-element.192, bf16[4096,1024]{1,0:T(8,128)(2,1)} %all-gather.18.cloned.1.call-done, f32[1024]{0:T(1024)S(1)} %bitcast.258, f32[]{:T(128)} %bitcast.22), kind=kOutput, calls=%fused_computation.111 | convolution fusion | flops 9265545216 | bytes 24219652 | tf_op jit(solution)/shard_map/dot_general | solution.py:23
  1227.4 85.5 %all-reduce.13.cloned.1.call-done = (bf16[256,3072]{1,0:T(8,128)(2,1)}, bf16[256,1024]{1,0:T(8,128)(2,1)}, bf16[256,4096]{1,0:T(8,128)(2,1)}, bf16[1024,1024]{1,0:T(8,128)(2,1)}) async-done(((bf16[256,3072]{1,0:T(8,128)(2,1)}, bf16[256,1024]{1,0:T(8,128)(2,1)}, bf16[256,4096]{1,0:T(8,128)(2,1)}, bf16[1024,1024]{1,0:T(8,128)(2,1)}), (bf16[256,3072]{1,0:T(8,128)(2,1)}, bf16[256,1024]{1,0:T(8,128)(2,1)}, ...) | async-done | bytes 6291472 | tf_op jit(solution)/shard_map/psum | solution.py:257
  (295 shorter events, 467.9 us)
Async XLA Ops:
  7.2 72.2 %copy-start.47 = (bf16[1024]{0:T(1024)(128)(2,1)S(1)}, bf16[1024]{0:T(1024)(128)(2,1)}, u32[]{:S(2)}) copy-start(bf16[1024]{0:T(1024)(128)(2,1)} %param.30) | copy-start | bytes 6148
  7.3 88.8 %copy-start.3 = (bf16[1,1,1104,1024]{3,2,1,0:T(8,128)(2,1)S(1)}, bf16[1,1,1104,1024]{3,2,1,0:T(8,128)(2,1)}, u32[]{:S(2)}) copy-start(bf16[1,1,1104,1024]{3,2,1,0:T(8,128)(2,1)} %param.19) | copy-start | bytes 6782980
  7.3 120.9 %all-gather.12.cloned.1.call-start = ((), (), s32[]{:S(2)}) async-start(), calls=%async_computation.4 | async-start | bytes 7864320 | tf_op jit(solution)/shard_map/all_gather | solution.py:58
  8.0 279.7 %all-gather.14.cloned.1.call-start = ((), (), s32[]{:S(2)}) async-start(), calls=%async_computation.5 | async-start | bytes 2621440 | tf_op jit(solution)/shard_map/all_gather | solution.py:60
  8.7 315.1 %all-gather.16.cloned.1.call-start = ((), (), s32[]{:S(2)}) async-start(), calls=%async_computation.6 | async-start | bytes 10485760 | tf_op jit(solution)/shard_map/all_gather | solution.py:64
  9.5 463.7 %all-gather.18.cloned.1.call-start = ((), (), s32[]{:S(2)}) async-start(), calls=%async_computation.7 | async-start | bytes 10485760 | tf_op jit(solution)/shard_map/all_gather | solution.py:66
  10.1 901.8 %reduce-scatter.7.cloned.1.call-start = ((), (), s32[]{:S(2)}) async-start(), calls=%async_computation.9 | async-start | bytes 2621440 | tf_op jit(solution)/shard_map/reduce_scatter | solution.py:228
  53.3 84.6 %copy-start.44 = (f32[4,1,256]{2,1,0:T(1,128)}, f32[4,1,256]{2,1,0:T(1,128)S(1)}, u32[]{:S(2)}) copy-start(f32[4,1,256]{2,1,0:T(1,128)S(1)} %convert_element_type.230) | copy-start | bytes 12292
  67.3 70.5 %copy-start.33 = (f32[4,1,256]{2,1,0:T(1,128)}, f32[4,1,256]{2,1,0:T(1,128)S(1)}, u32[]{:S(2)}) copy-start(f32[4,1,256]{2,1,0:T(1,128)S(1)} %convert_element_type.229) | copy-start | bytes 12292
  96.4 41.4 %copy-start.21 = (f32[1104]{0:T(1024)}, f32[1104]{0:T(1024)S(1)}, u32[]{:S(2)}) copy-start(f32[1104]{0:T(1024)S(1)} %broadcast_multiply_fusion.1) | copy-start | bytes 13252
  97.8 40.1 %copy-start.23 = (f32[1104]{0:T(1024)}, f32[1104]{0:T(1024)S(1)}, u32[]{:S(2)}) copy-start(f32[1104]{0:T(1024)S(1)} %fusion.75) | copy-start | bytes 13252
  156.2 131.5 %copy-start.46 = (f32[4,1,256]{2,1,0:T(1,128)S(1)}, f32[4,1,256]{2,1,0:T(1,128)}, u32[]{:S(2)}) copy-start(f32[4,1,256]{2,1,0:T(1,128)} %convert_element_type.232) | copy-start | bytes 12292
  294.6 222.1 %copy-start.25 = (f32[1104]{0:T(1024)}, f32[1104]{0:T(1024)S(1)}, u32[]{:S(2)}) copy-start(f32[1104]{0:T(1024)S(1)} %broadcast_multiply_fusion) | copy-start | bytes 13252
  297.9 218.8 %copy-start.35 = (f32[1104]{0:T(1024)}, f32[1104]{0:T(1024)S(1)}, u32[]{:S(2)}) copy-start(f32[1104]{0:T(1024)S(1)} %fusion.76) | copy-start | bytes 13252
  323.9 149.3 %copy-start.6 = (bf16[1,1,1104,1024]{3,2,1,0:T(8,128)(2,1)S(1)}, bf16[1,1,1104,1024]{3,2,1,0:T(8,128)(2,1)}, u32[]{:S(2)}) copy-start(bf16[1,1,1104,1024]{3,2,1,0:T(8,128)(2,1)} %param.33) | copy-start | bytes 6782980
  526.0 385.8 %reduce-scatter.5.cloned.1.call-start = ((), (), s32[]{:S(2)}) async-start(), calls=%async_computation.8 | async-start | bytes 7864320 | tf_op jit(solution)/shard_map/reduce_scatter | solution.py:222
  538.8 243.8 %copy-start.22 = (f32[1104]{0:T(1024)S(1)}, f32[1104]{0:T(1024)}, u32[]{:S(2)}) copy-start(f32[1104]{0:T(1024)} %copy-done.21) | copy-start | bytes 13252
  538.8 243.8 %copy-start.24 = (f32[1104]{0:T(1024)S(1)}, f32[1104]{0:T(1024)}, u32[]{:S(2)}) copy-start(f32[1104]{0:T(1024)} %copy-done.23) | copy-start | bytes 13252
  538.8 243.8 %copy-start.34 = (f32[4,1,256]{2,1,0:T(1,128)S(1)}, f32[4,1,256]{2,1,0:T(1,128)}, u32[]{:S(2)}) copy-start(f32[4,1,256]{2,1,0:T(1,128)} %copy-done.33) | copy-start | bytes 12292
  538.8 243.8 %copy-start.45 = (f32[4,1,256]{2,1,0:T(1,128)S(1)}, f32[4,1,256]{2,1,0:T(1,128)}, u32[]{:S(2)}) copy-start(f32[4,1,256]{2,1,0:T(1,128)} %copy-done.44) | copy-start | bytes 12292
  797.9 257.7 %reduce-scatter.9.cloned.1.call-start = ((), (), s32[]{:S(2)}) async-start(), calls=%async_computation.10 | async-start | bytes 10485760 | tf_op jit(solution)/shard_map/reduce_scatter | solution.py:240
  817.3 386.0 %reduce-scatter.11.cloned.1.call-start = ((), (), s32[]{:S(2)}) async-start(), calls=%async_computation.11 | async-start | bytes 10485760 | tf_op jit(solution)/shard_map/reduce_scatter | solution.py:246
  836.3 476.6 %all-reduce.13.cloned.1.call-start = ((), (), s32[]{:S(2)}) async-start(), calls=%async_computation.12 | async-start | bytes 12582912 | tf_op jit(solution)/shard_map/psum | solution.py:257
  872.0 331.4 %copy-start.32 = (f32[1104]{0:T(1024)S(1)}, f32[1104]{0:T(1024)}, u32[]{:S(2)}) copy-start(f32[1104]{0:T(1024)} %copy-done.31) | copy-start | bytes 13252
  (64 other events, 476.7 us)
Sparse Core Ops, SparseCore 0:
  9.7 118.4 all-gather.11
  129.7 44.1 all-gather.13
  175.5 148.3 all-gather.15
  325.3 147.8 all-gather.17
  526.1 42.0 reduce-scatter.6
  798.1 110.0 reduce-scatter.4
  910.7 144.9 reduce-scatter.8
  1058.1 145.1 reduce-scatter.10
  1207.4 105.4 all-reduce.12
where the time goes:
time: 1340 us; the launch traced here: 1330 us
  waiting for transfers between devices  531 us (40%)
  matrix products  475 us (35%)
  other arithmetic  137 us (10%)
  blocking collectives  125 us (9%)
  local copies, waits for them, and re-layouts  42.8 us (3%)
  between operations  17.3 us (1%)
    reduce_scatter x1, waiting for transfers between devices, body(): lax.psum_scatter(grad_wdown.astype(jnp.bfloat16), 'shard', scatter_dimens...  148 us
    reduce_scatter x1, waiting for transfers between devices, body(): lax.psum_scatter(grad_wup.astype(jnp.bfloat16), 'shard', scatter_dimensio...  144 us
    all_gather x1, waiting for transfers between devices, body(): lax.all_gather(w_down, 'shard', axis=0, tiled=True)  94.9 us
    dot_general x4, matrix products, matmul(): return jnp.dot(left, right, preferred_element_type=jnp.float32)  88.1 us
    psum x1, waiting for transfers between devices, body(): lax.psum(o_qkv.astype(jnp.bfloat16), 'rep').astype(jnp.float32)  85.5 us
    dot_general x4, matrix products, backward_group(): jnp.einsum('cqhd,ckhd->chqk', grad_part, value_part, preferred_element_ty...  70.2 us
    dot_general x4, matrix products, right_trans(): lax.dot_general(left, right, (((1,), (1,)), ((), ())), preferred_element_...  61 us
    dot_general x4, matrix products, left_trans(): lax.dot_general(left, right, (((0,), (0,)), ((), ())), preferred_element_...  55.5 us
  transfers between devices with their start and end apart: 9, of which 6 were waited for; matrix products, arithmetic and copies ran while one was open for 43% of the time, Pallas kernels for 0%

commit v1 on v0

--- a/solution.py
+++ b/solution.py
@@ -7,6 +7,27 @@
 HDIM = 64
 eps = 1e-06
 head_block = 4
+
+
+def joined_along(blocks, dim):
+    blocks = jnp.moveaxis(blocks, 0, dim)
+    shape = blocks.shape
+    return blocks.reshape(*shape[:dim], shape[dim] * shape[dim + 1], *shape[dim + 2 :])
+
+
+def grow_blocks(x, axis):
+    size, index = (lax.axis_size(axis), lax.axis_index(axis))
+    blocks, bit = (x[None], 1)
+    while bit < size:
+        other = lax.ppermute(blocks, axis, [(i, i ^ bit) for i in range(size)])
+        low = index & bit == 0
+        blocks = jnp.concatenate([jnp.where(low, blocks, other), jnp.where(low, other, blocks)])
+        bit *= 2
+    return blocks
+
+
+def doubled_up(x, axis, dim):
+    return joined_along(grow_blocks(x, axis), dim)
 
 
 def layer_norm(values, gain, shift):
@@ -63,7 +84,7 @@
         lax.all_gather(ln2_shift, "shard", axis=0, tiled=True),
         lax.all_gather(w_up, "shard", axis=0, tiled=True),
         lax.all_gather(up_bias, "shard", axis=0, tiled=True),
-        lax.all_gather(w_down, "shard", axis=0, tiled=True),
+        doubled_up(w_down, "shard", 0),
         lax.all_gather(down_bias, "shard", axis=0, tiled=True),
     )
     (

time: 1340 us -> 1540 us (1.15)
  blocking collectives: 125 us -> 286 us
  waiting for transfers between devices: 531 us -> 562 us
    ppermute x0 -> x2, waiting for transfers between devices: none -> 291 us  [grow_blocks(): other = lax.ppermute(blocks, axis, [(i, i ^ bit) for i in range(size)])]
    all_gather x1, blocking collectives: 8.1 us -> 172 us  [body(): lax.all_gather(down_bias, 'shard', axis=0, tiled=True)]
    reduce_scatter x1, waiting for transfers between devices: 144 us -> 0.01 us  [body(): lax.psum_scatter(grad_wup.astype(jnp.bfloat16), 'shard', scatter_dimensio...]
    reduce_scatter x1, waiting for transfers between devices: 148 us -> 29.8 us  [body(): lax.psum_scatter(grad_wdown.astype(jnp.bfloat16), 'shard', scatter_dimens...]
  transfers between devices with their start and end apart: 9 -> 11, of which waited for: 6 -> 7; matrix products, arithmetic and copies ran while one was open for 43% -> 38% of each run, Pallas kernels for 0% -> 0%
where the time goes in v1:
time: 1540 us; the launch traced here: 1530 us
  waiting for transfers between devices  562 us (36%)
  matrix products  474 us (31%)
  blocking collectives  286 us (19%)
  other arithmetic  152 us (10%)
  local copies, waits for them, and re-layouts  41.8 us (3%)
  between operations  17.4 us (1%)
    ppermute x2, waiting for transfers between devices, grow_blocks(): other = lax.ppermute(blocks, axis, [(i, i ^ bit) for i in range(size)])  291 us
    all_gather x1, blocking collectives, body(): lax.all_gather(down_bias, 'shard', axis=0, tiled=True)  172 us
    all_gather x1, waiting for transfers between devices, body(): lax.all_gather(w_down, 'shard', axis=0, tiled=True)  95 us
    dot_general x4, matrix products, matmul(): return jnp.dot(left, right, preferred_element_type=jnp.float32)  87.5 us
    psum x1, waiting for transfers between devices, body(): lax.psum(o_qkv.astype(jnp.bfloat16), 'rep').astype(jnp.float32)  82.6 us
    dot_general x4, matrix products, backward_group(): jnp.einsum('cqhd,ckhd->chqk', grad_part, value_part, preferred_element_ty...  66.7 us
    dot_general x4, matrix products, right_trans(): lax.dot_general(left, right, (((1,), (1,)), ((), ())), preferred_element_...  61 us
    dot_general x4, matrix products, left_trans(): lax.dot_general(left, right, (((0,), (0,)), ((), ())), preferred_element_...  55.6 us
  transfers between devices with their start and end apart: 11, of which 7 were waited for; matrix products, arithmetic and copies ran while one was open for 38% of the time, Pallas kernels for 0%

profile of v1, /device:TPU:0, one launch (start us, length us, event | category | flops | bytes accessed | tf_op | source)
XLA Modules:
  0.0 1534.4 jit_solution(9716562958817226974)
XLA Ops:
  63.7 15.2 all-gather.5
  79.4 16.0 %all_gather.48 = bf16[4096]{0:T(1024)(128)(2,1)S(1)} all-gather(bf16[1024]{0:T(1024)(128)(2,1)S(1)} %copy-done.48), channel_id=1, replica_groups=mesh['rep'=8,'shard'=4] {'shard'}, dimensions={0}, use_global_device_ids=true | all-gather | bytes 10240 | tf_op jit(solution)/shard_map/all_gather | solution.py:86
  96.6 31.5 %all-gather.12.cloned.1.call-done = bf16[1024,3072]{1,0:T(8,128)(2,1)} async-done(((bf16[256,3072]{1,0:T(8,128)(2,1)}), bf16[1024,3072]{1,0:T(8,128)(2,1)}) %all-gather.12.cloned.1.call-update) | async-done | bytes 6291472 | tf_op jit(solution)/shard_map/all_gather | solution.py:79
  153.7 130.5 %while.26 = (s32[]{:T(128)}, bf16[4,1,1104,4,64]{2,4,3,1,0:T(8,128)(2,1)}, f32[4,1,4,1104]{3,2,1,0:T(4,128)}, bf16[4,1,1104,4,64]{2,4,3,1,0:T(8,128)(2,1)}, bf16...) while((s32[]{:T(128)}, bf16[4,1,1104,4,64]{2,4,3,1,0:T(8,128)(2,1)}, ...), condition=%wide.region_5.6_spmd, body=%wide.region_2.5_spmd.sunk | while | flops 1282190080 | bytes 62444876 | solution.py:149
  294.4 29.4 %all-gather.16.cloned.1.call-done = bf16[1024,4096]{1,0:T(8,128)(2,1)} async-done(((bf16[256,4096]{1,0:T(8,128)(2,1)}), bf16[1024,4096]{1,0:T(8,128)(2,1)}) %all-gather.16.cloned.1.call-update) | async-done | bytes 8388624 | tf_op jit(solution)/shard_map/all_gather | solution.py:85
  323.9 54.4 %multiply_convert_fusion.1 = (bf16[1104,4096]{1,0:T(8,128)(2,1)}, f32[1104,4096]{1,0:T(8,128)}, f32[1104,4096]{1,0:T(8,128)}) fusion(f32[4096]{0:T(1024)S(1)} %copy-done.40, bf16[1024,4096]{1,0:T(8,128)(2,1)} %all-gather.16.cloned.1.call-done, f32[1104,1024]{1,0:T(8,128)} %copy-done.10, f32[1024]{0:T(1024)S(1)} %bitcast.262, f32[1024]{0:T(1024)S(1)} %bitcast.254, ...), kind=kOutput, calls=%fused_computation.56 | convolution fusion | flops 9565126656 | bytes 58163840 | tf_op jit(solution)/shard_map/dot_general | solution.py:44
  378.2 95.0 %all-gather.18.cloned.1.call-done = bf16[4096,1024]{1,0:T(8,128)(2,1)} async-done(((bf16[1024,1024]{1,0:T(8,128)(2,1)}), bf16[4096,1024]{1,0:T(8,128)(2,1)}) %all-gather.18.cloned.1.call-update) | async-done | bytes 8388624 | tf_op jit(solution)/shard_map/all_gather | solution.py:172
  473.2 25.4 %fusion.92 = (bf16[4096]{0:T(1024)(128)(2,1)}, bf16[1104,4096]{1,0:T(8,128)(2,1)}) fusion(f32[1104,4096]{1,0:T(8,128)} %get-tuple-element.193, f32[1104,4096]{1,0:T(8,128)} %get-tuple-element.210, bf16[4096,1024]{1,0:T(8,128)(2,1)} %all-gather.18.cloned.1.call-done, bf16[1,1,1104,1024]{3,2,1,0:T(8,128)(2,1)S(1)} %copy-done.6, f32[]{:T(128)} %bitcast.22), kind=kOutput, calls=%fused_computation.143 | convolution fusion | flops 9332240384 | bytes 55877636 | tf_op jit(solution)/shard_map/dot_general | solution.py:54
  498.6 18.1 %multiply_reduce_fusion.1 = (bf16[1024]{0:T(1024)(128)(2,1)}, f32[1104]{0:T(1024)S(1)}, bf16[1024]{0:T(1024)(128)(2,1)}, f32[1104,1024]{1,0:T(8,128)S(1)}) fusion(f32[1104,1024]{1,0:T(8,128)} %copy-done.10, f32[1104]{0:T(1024)S(1)} %fusion.76, f32[1104]{0:T(1024)S(1)} %broadcast_multiply_fusion, f32[1024]{0:T(1024)S(1)} %bitcast.255, ...), kind=kOutput, calls=%fused_computation.103 | convolution fusion | flops 9270064128 | bytes 26497984 | tf_op jit(solution)/shard_map/dot_general | solution.py:54
  538.7 243.3 %while.27 = (s32[]{:T(128)}, bf16[4,1,1104,4,64]{2,4,3,1,0:T(8,128)(2,1)}, bf16[4,1,1104,4,64]{2,4,3,1,0:T(8,128)(2,1)}, bf16[4,1,1104,4,64]{2,4,3,1,0:T(8,128)(...) while((s32[]{:T(128)}, ...), condition=%wide.region_12.13_spmd, body=%wide.region_10.12_spmd.sunk | while | flops 3159731968 | bytes 201783552 | solution.py:224
  550.6 16.8 %multiply_reduce_fusion.5 = (f32[4,1104]{1,0:T(4,128)S(1)}, f32[4,1104,1104]{1,2,0:T(8,128)}) fusion(f32[4,1104,1104]{1,2,0:T(8,128)} %fusion.140, bf16[4,1,1104,4,64]{2,4,3,1,0:T(8,128)(2,1)} %get-tuple-element.364, s32[]{:T(128)} %get-tuple-element.346, bf16[4,1,1104,4,64]{2,4,3,1,0:T(8,128)(2,1)S(1)} %copy-done.5), kind=kOutput, calls=%fused_computation.20.clone.1 | convolution fusion | flops 633779904 | bytes 41048320 | tf_op jit(solution)/shard_map/while/body/eval_jaxpr/cqhd,ckhd->chqk/dot_general | solution.py:204
  611.4 16.6 %multiply_reduce_fusion.5 = (f32[4,1104]{1,0:T(4,128)S(1)}, f32[4,1104,1104]{1,2,0:T(8,128)}) fusion(f32[4,1104,1104]{1,2,0:T(8,128)} %fusion.140, bf16[4,1,1104,4,64]{2,4,3,1,0:T(8,128)(2,1)} %get-tuple-element.364, s32[]{:T(128)} %get-tuple-element.346, bf16[4,1,1104,4,64]{2,4,3,1,0:T(8,128)(2,1)S(1)} %copy-done.5), kind=kOutput, calls=%fused_computation.20.clone.1 | convolution fusion | flops 633779904 | bytes 41048320 | tf_op jit(solution)/shard_map/while/body/eval_jaxpr/cqhd,ckhd->chqk/dot_general | solution.py:204
  672.2 16.6 %multiply_reduce_fusion.5 = (f32[4,1104]{1,0:T(4,128)S(1)}, f32[4,1104,1104]{1,2,0:T(8,128)}) fusion(f32[4,1104,1104]{1,2,0:T(8,128)} %fusion.140, bf16[4,1,1104,4,64]{2,4,3,1,0:T(8,128)(2,1)} %get-tuple-element.364, s32[]{:T(128)} %get-tuple-element.346, bf16[4,1,1104,4,64]{2,4,3,1,0:T(8,128)(2,1)S(1)} %copy-done.5), kind=kOutput, calls=%fused_computation.20.clone.1 | convolution fusion | flops 633779904 | bytes 41048320 | tf_op jit(solution)/shard_map/while/body/eval_jaxpr/cqhd,ckhd->chqk/dot_general | solution.py:204
  732.9 16.6 %multiply_reduce_fusion.5 = (f32[4,1104]{1,0:T(4,128)S(1)}, f32[4,1104,1104]{1,2,0:T(8,128)}) fusion(f32[4,1104,1104]{1,2,0:T(8,128)} %fusion.140, bf16[4,1,1104,4,64]{2,4,3,1,0:T(8,128)(2,1)} %get-tuple-element.364, s32[]{:T(128)} %get-tuple-element.346, bf16[4,1,1104,4,64]{2,4,3,1,0:T(8,128)(2,1)S(1)} %copy-done.5), kind=kOutput, calls=%fused_computation.20.clone.1 | convolution fusion | flops 633779904 | bytes 41048320 | tf_op jit(solution)/shard_map/while/body/eval_jaxpr/cqhd,ckhd->chqk/dot_general | solution.py:204
  782.0 15.5 %convolution_convert_fusion.2 = bf16[1024,3072]{1,0:T(8,128)(2,1)} fusion(bf16[1,1,1104,1024]{3,2,1,0:T(8,128)(2,1)} %param.19, f32[1024]{0:T(1024)S(1)} %bitcast.261, f32[1024]{0:T(1024)S(1)} %bitcast.250, f32[1104]{0:T(1024)S(1)} %copy-done.25, f32[1104]{0:T(1024)S(1)} %copy-done.23, bf16[1104,1024]{0,1:T(8,128)(2,1)} %bitcast.242, ...), kind=kOutput, calls=%fused_computation.76 | convolution fusion | flops 6976045056 | bytes 15352448 | tf_op jit(solution)/shard_map/dot_general | solution.py:48
  798.3 18.5 %convolution_convert_fusion.1 = bf16[1024,4096]{1,0:T(8,128)(2,1)} fusion(bf16[1104,4096]{1,0:T(8,128)(2,1)} %get-tuple-element.214, f32[1104,1024]{1,0:T(8,128)} %copy-done.10, f32[1024]{0:T(1024)S(1)} %bitcast.263, f32[1024]{0:T(1024)S(1)} %bitcast.257, f32[1104]{0:T(1024)S(1)} %copy-done.37, f32[1104]{0:T(1024)S(1)} %copy-done.27), kind=kOutput, calls=%fused_computation.72 | convolution fusion | flops 9270870016 | bytes 21971584 | tf_op jit(solution)/shard_map/dot_general | solution.py:48
  818.4 17.4 %convolution_convert_fusion = bf16[4096,1024]{1,0:T(8,128)(2,1)} fusion(bf16[1104,4096]{1,0:T(8,128)(2,1)} %get-tuple-element.192, bf16[1,1,1104,1024]{3,2,1,0:T(8,128)(2,1)S(1)} %copy-done.7, f32[]{:T(128)} %bitcast.22), kind=kOutput, calls=%fused_computation.71 | convolution fusion | flops 9268609024 | bytes 19693572 | tf_op jit(solution)/shard_map/dot_general | solution.py:48
  836.0 114.2 %collective-permute-done = bf16[1,1024,1024]{2,1,0:T(8,128)(2,1)} collective-permute-done((bf16[1,1024,1024]{2,1,0:T(8,128)(2,1)}, bf16[1,1024,1024]{2,1,0:T(8,128)(2,1)}, u32[]{:S(2)}, u32[]{:S(2)}) %collective-permute-start) | collective-permute-done | bytes 2097184 | tf_op jit(solution)/shard_map/ppermute | solution.py:22
  959.0 172.2 %all-gather.6 = bf16[4,1,256]{2,1,0:T(2,128)(2,1)S(1)} all-gather(bf16[1,1,256]{2,1,0:T(2,128)(2,1)S(1)} %reshape.276), channel_id=1, replica_groups=mesh['rep'=8,'shard'=4] {'shard'}, dimensions={0}, use_global_device_ids=true | all-gather | bytes 2560 | tf_op jit(solution)/shard_map/all_gather | solution.py:88
  1131.7 177.0 %collective-permute-done.1 = bf16[2,1024,1024]{2,1,0:T(8,128)(2,1)} collective-permute-done((bf16[2,1024,1024]{2,1,0:T(8,128)(2,1)}, bf16[2,1024,1024]{2,1,0:T(8,128)(2,1)}, u32[]{:S(2)}, u32[]{:S(2)}) %collective-permute-start.1) | collective-permute-done | bytes 4194336 | tf_op jit(solution)/shard_map/ppermute | solution.py:22
  1344.4 19.4 %all-reduce.10 = (bf16[1024]{0:T(1024)(128)(2,1)S(1)}, bf16[1024]{0:T(1024)(128)(2,1)S(1)}, bf16[2048]{0:T(1024)(128)(2,1)S(1)}, bf16[1024]{0:T(1024)(128)(2,1)S...) all-reduce(bf16[1024]{0:T(1024)(128)(2,1)S(1)} %get-tuple-element.1, ...), channel_id=2, replica_groups=mesh['rep'=8,'shard'=4] {'shard'}, use_global_device_ids=true, to_apply=%region_16.17.clone | all-reduce | flops 12288 | bytes 49152
  1382.0 29.8 %reduce-scatter.11.cloned.1.call-done = bf16[1024,1024]{1,0:T(8,128)(2,1)} async-done(((bf16[4096,1024]{1,0:T(8,128)(2,1)}), bf16[1024,1024]{1,0:T(8,128)(2,1)}) %reduce-scatter.11.cloned.1.call-update) | async-done | bytes 2097168 | tf_op jit(solution)/shard_map/reduce_scatter | solution.py:267
  1418.5 16.6 %fusion.72 = bf16[1,1,1104,1024]{3,2,1,0:T(8,128)(2,1)} fusion(f32[1104,1024]{1,0:T(8,128)} %copy-done.10, bf16[1104,4096]{1,0:T(8,128)(2,1)} %get-tuple-element.192, bf16[4096,1024]{1,0:T(8,128)(2,1)} %bitcast.245, f32[1024]{0:T(1024)S(1)} %bitcast.264, f32[]{:T(128)} %bitcast.22), kind=kOutput, calls=%fused_computation.115 | convolution fusion | flops 9265545216 | bytes 24219652 | tf_op jit(solution)/shard_map/dot_general | solution.py:44
  1435.2 82.6 %all-reduce.13.cloned.1.call-done = (bf16[256,3072]{1,0:T(8,128)(2,1)}, bf16[256,1024]{1,0:T(8,128)(2,1)}, bf16[256,4096]{1,0:T(8,128)(2,1)}, bf16[1024,1024]{1,0:T(8,128)(2,1)}) async-done(((bf16[256,3072]{1,0:T(8,128)(2,1)}, bf16[256,1024]{1,0:T(8,128)(2,1)}, bf16[256,4096]{1,0:T(8,128)(2,1)}, bf16[1024,1024]{1,0:T(8,128)(2,1)}), (bf16[256,3072]{1,0:T(8,128)(2,1)}, bf16[256,1024]{1,0:T(8,128)(2,1)}, ...) | async-done | bytes 6291472 | tf_op jit(solution)/shard_map/psum | solution.py:278
  (293 shorter events, 501.3 us)
Async XLA Ops:
  7.2 121.0 %all-gather.12.cloned.1.call-start = ((), (), s32[]{:S(2)}) async-start(), calls=%async_computation.4 | async-start | bytes 7864320 | tf_op jit(solution)/shard_map/all_gather | solution.py:79
  7.9 276.3 %all-gather.14.cloned.1.call-start = ((), (), s32[]{:S(2)}) async-start(), calls=%async_computation.5 | async-start | bytes 2621440 | tf_op jit(solution)/shard_map/all_gather | solution.py:81
  8.7 70.7 %copy-start.48 = (bf16[1024]{0:T(1024)(128)(2,1)S(1)}, bf16[1024]{0:T(1024)(128)(2,1)}, u32[]{:S(2)}) copy-start(bf16[1024]{0:T(1024)(128)(2,1)} %param.30) | copy-start | bytes 6148
  8.7 315.1 %all-gather.16.cloned.1.call-start = ((), (), s32[]{:S(2)}) async-start(), calls=%async_computation.6 | async-start | bytes 10485760 | tf_op jit(solution)/shard_map/all_gather | solution.py:85
  9.5 463.7 %all-gather.18.cloned.1.call-start = ((), (), s32[]{:S(2)}) async-start(), calls=%async_computation.7 | async-start | bytes 10485760 | tf_op jit(solution)/shard_map/all_gather | solution.py:172
  10.1 1371.9 %reduce-scatter.7.cloned.1.call-start = ((), (), s32[]{:S(2)}) async-start(), calls=%async_computation.9 | async-start | bytes 2621440 | tf_op jit(solution)/shard_map/reduce_scatter | solution.py:249
  10.5 127.3 %copy-start.22 = (f32[1104]{0:T(1024)}, f32[1104]{0:T(1024)S(1)}, u32[]{:S(2)}) copy-start(f32[1104]{0:T(1024)S(1)} %broadcast_multiply_fusion.1) | copy-start | bytes 13252
  11.9 126.0 %copy-start.24 = (f32[1104]{0:T(1024)}, f32[1104]{0:T(1024)S(1)}, u32[]{:S(2)}) copy-start(f32[1104]{0:T(1024)S(1)} %fusion.75) | copy-start | bytes 13252
  24.5 113.4 %copy-start.34 = (f32[4,1,256]{2,1,0:T(1,128)}, f32[4,1,256]{2,1,0:T(1,128)S(1)}, u32[]{:S(2)}) copy-start(f32[4,1,256]{2,1,0:T(1,128)S(1)} %convert_element_type.229) | copy-start | bytes 12292
  32.3 105.6 %copy-start.43 = (f32[4,1,256]{2,1,0:T(1,128)}, f32[4,1,256]{2,1,0:T(1,128)S(1)}, u32[]{:S(2)}) copy-start(f32[4,1,256]{2,1,0:T(1,128)S(1)} %convert_element_type.230) | copy-start | bytes 12292
  153.7 130.5 %copy-start.47 = (f32[4,1,256]{2,1,0:T(1,128)S(1)}, f32[4,1,256]{2,1,0:T(1,128)}, u32[]{:S(2)}) copy-start(f32[4,1,256]{2,1,0:T(1,128)} %convert_element_type.232) | copy-start | bytes 12292
  291.2 225.5 %copy-start.26 = (f32[1104]{0:T(1024)}, f32[1104]{0:T(1024)S(1)}, u32[]{:S(2)}) copy-start(f32[1104]{0:T(1024)S(1)} %broadcast_multiply_fusion) | copy-start | bytes 13252
  294.4 222.3 %copy-start.36 = (f32[1104]{0:T(1024)}, f32[1104]{0:T(1024)S(1)}, u32[]{:S(2)}) copy-start(f32[1104]{0:T(1024)S(1)} %fusion.76) | copy-start | bytes 13252
  323.8 149.3 %copy-start.6 = (bf16[1,1,1104,1024]{3,2,1,0:T(8,128)(2,1)S(1)}, bf16[1,1,1104,1024]{3,2,1,0:T(8,128)(2,1)}, u32[]{:S(2)}) copy-start(bf16[1,1,1104,1024]{3,2,1,0:T(8,128)(2,1)} %param.33) | copy-start | bytes 6782980
  526.0 856.0 %reduce-scatter.5.cloned.1.call-start = ((), (), s32[]{:S(2)}) async-start(), calls=%async_computation.8 | async-start | bytes 7864320 | tf_op jit(solution)/shard_map/reduce_scatter | solution.py:243
  538.7 243.3 %copy-start.23 = (f32[1104]{0:T(1024)S(1)}, f32[1104]{0:T(1024)}, u32[]{:S(2)}) copy-start(f32[1104]{0:T(1024)} %copy-done.22) | copy-start | bytes 13252
  538.7 243.3 %copy-start.25 = (f32[1104]{0:T(1024)S(1)}, f32[1104]{0:T(1024)}, u32[]{:S(2)}) copy-start(f32[1104]{0:T(1024)} %copy-done.24) | copy-start | bytes 13252
  538.7 243.3 %copy-start.35 = (f32[4,1,256]{2,1,0:T(1,128)S(1)}, f32[4,1,256]{2,1,0:T(1,128)}, u32[]{:S(2)}) copy-start(f32[4,1,256]{2,1,0:T(1,128)} %copy-done.34) | copy-start | bytes 12292
  538.7 243.3 %copy-start.44 = (f32[4,1,256]{2,1,0:T(1,128)S(1)}, f32[4,1,256]{2,1,0:T(1,128)}, u32[]{:S(2)}) copy-start(f32[4,1,256]{2,1,0:T(1,128)} %copy-done.43) | copy-start | bytes 12292
  797.6 584.4 %reduce-scatter.9.cloned.1.call-start = ((), (), s32[]{:S(2)}) async-start(), calls=%async_computation.10 | async-start | bytes 10485760 | tf_op jit(solution)/shard_map/reduce_scatter | solution.py:261
  816.8 595.0 %reduce-scatter.11.cloned.1.call-start = ((), (), s32[]{:S(2)}) async-start(), calls=%async_computation.11 | async-start | bytes 10485760 | tf_op jit(solution)/shard_map/reduce_scatter | solution.py:267
  835.8 682.0 %all-reduce.13.cloned.1.call-start = ((), (), s32[]{:S(2)}) async-start(), calls=%async_computation.12 | async-start | bytes 12582912 | tf_op jit(solution)/shard_map/psum | solution.py:278
  835.9 114.3 %collective-permute-start = (bf16[1,1024,1024]{2,1,0:T(8,128)(2,1)}, bf16[1,1024,1024]{2,1,0:T(8,128)(2,1)}, u32[]{:S(2)}, u32[]{:S(2)}) collective-permute-start(bf16[1,1024,1024]{2,1,0:T(8,128)(2,1)} %bitcast.246), channel_id=1, source_target_pairs={{0,1},{1,0},{2,3},{3,2},{4,5},{5,4},{6,7},{7,6},{8,9},{9,8},{10,11... | collective-permute-start | bytes 6291464 | tf_op jit(solution)/shard_map/ppermute | solution.py:22
  956.4 352.4 %collective-permute-start.1 = (bf16[2,1024,1024]{2,1,0:T(8,128)(2,1)}, bf16[2,1024,1024]{2,1,0:T(8,128)(2,1)}, u32[]{:S(2)}, u32[]{:S(2)}) collective-permute-start(bf16[2,1024,1024]{2,1,0:T(8,128)(2,1)} %pad_maximum_fusion.2), channel_id=1, source_target_pairs={{0,2},{1,3},{2,0},{3,1},{4,6},{5,7},{6,4},{7,5},{8,10},{9,11},{10,... | collective-permute-start | bytes 12582920 | tf_op jit(solution)/shard_map/ppermute | solution.py:22
  (61 other events, 609.7 us)
Sparse Core Ops, SparseCore 0:
  9.6 118.5 all-gather.11
  129.8 44.0 all-gather.13
  175.5 148.3 all-gather.15
  325.3 147.8 all-gather.17
  526.1 42.0 reduce-scatter.6
  797.7 152.0 reduce-scatter.4
  952.3 286.6 reduce-scatter.8
  1241.4 170.2 reduce-scatter.10
  1415.8 101.9 all-reduce.12
